TPU v7x, 512 devices: a whole 4x4x16 slice. The times are simulated.
512 devices in a mesh: row: 32 (over z, core), col: 16 (over y, x).
Axes of the slice: x: 4, y: 4, z: 16, core: 2. Of those that a mesh axis runs over, the one named last changes fastest.
Arguments:
- features: bfloat16 [16, 4096, 256], P('col', 'row'), may hold values from -6 to 6
- tiles: bfloat16 [32, 16, 56, 128, 128], P('row', 'col'), may hold values from -0.5 to 0.5
- tile_rows: int32 [32, 16, 56], P('row', 'col'), may hold values from 0 to 15, as said below
- tile_cols: int32 [32, 16, 56], P('row', 'col'), may hold values from 0 to 31, as said below
- tile_count: int32 [32, 16], P('row', 'col'), may hold values from 4 to 56, as said below
- weight: bfloat16 [256, 256], replicated, may hold values from -0.375 to 0.375
- bias: float32 [256], replicated, may hold values from -3 to 3
- cotangent: bfloat16 [32, 2048, 256], P('row', 'col'), may hold values from -6 to 6
- label_mask: int32 [32, 2048], P('row', 'col'), may hold values 0 or 1
Outputs:
- hidden: bfloat16 [32, 2048, 256], P('row', 'col')
- grad_weight: float32 [256, 256], replicated
- grad_bias: float32 [256], replicated
- grad_features: bfloat16 [16, 4096, 256], P('col', 'row')
Inputs may be any that keep to these rules, and one draw needn't show every extreme that they name: `tile_rows`: tile row among the 16 tile rows of a block; the (row, column) positions of one block's slots are all distinct. `tile_cols`: tile column among the 32 tile columns of a block. The live slots of a block are its first tile_count slots; some block has all 56 slots live.
All inputs are finite; a program needn't handle non-finite values. No bound on the sum of `label_mask` on one device may be relied on, other than what follows from the above.
Results may differ from a plain program's by a relative error of at most 0.023.
Values may be sent and summed in bfloat16 or wider, within the bound.
A program may use at most 64 MiB of HBM per device.

v0:
```python
import math
import jax
import jax.numpy as jnp
from jax import lax
from jax.sharding import PartitionSpec as P


def tile_products(block_tiles, take_index, put_index, live_count, source, out_tiles, transpose):
    total_slots = block_tiles.shape[0]
    group = math.gcd(total_slots, 16)
    tile_size = block_tiles.shape[1]
    width = source.shape[-1]
    form = "sij,sif->sjf" if transpose else "sij,sjf->sif"

    def step(turn, accum):
        start = turn * group
        block = lax.dynamic_slice_in_dim(block_tiles, start, group, 0)
        take = lax.dynamic_slice_in_dim(take_index, start, group, 0)
        put = lax.dynamic_slice_in_dim(put_index, start, group, 0)
        live = start + jnp.arange(group, dtype=jnp.int32) < live_count
        picked = jnp.take(source, take, axis=0)
        product = jnp.einsum(form, block, picked, preferred_element_type=jnp.float32)
        product = jnp.where(live[:, None, None], product, 0.0)
        return accum.at[put].add(product)

    turns = (live_count + group - 1) // group
    start_value = jnp.zeros((out_tiles, tile_size, width), jnp.float32)
    return lax.fori_loop(0, turns, step, start_value)


def times_weight_t(values, weight):
    return lax.dot_general(
        values, weight, (((1,), (1,)), ((), ())), preferred_element_type=jnp.float32
    ).astype(jnp.bfloat16)


def on_device(
    features, tiles, tile_rows, tile_cols, tile_count, weight, bias, cotangent, label_mask
):
    tile_size = tiles.shape[-1]
    rows_dev = features.shape[1]
    width = features.shape[2]
    n_row = lax.axis_size("row")
    n_col = lax.axis_size("col")
    own_tiles = tiles[0, 0]
    rows_index = tile_rows[0, 0]
    cols_index = tile_cols[0, 0]
    live_count = tile_count[0, 0]
    gathered = lax.all_gather(features, "row", axis=1, tiled=True)
    source = gathered.reshape(n_row * rows_dev // tile_size, tile_size, width)
    partial_value = tile_products(
        own_tiles, cols_index, rows_index, live_count, source, n_col * rows_dev // tile_size, False
    )
    partial_value = partial_value.reshape(n_col * rows_dev, width)
    summed = lax.psum_scatter(
        partial_value.astype(jnp.bfloat16), "col", scatter_dimension=0, tiled=True
    )
    pre_act = jnp.dot(summed, weight, preferred_element_type=jnp.float32) + bias
    sigma = jax.nn.sigmoid(pre_act)
    hidden = (pre_act * sigma).astype(jnp.bfloat16)
    kept = label_mask[0].astype(jnp.float32)[:, None]
    slope = sigma * (1.0 + pre_act * (1.0 - sigma))
    grad_pre = (cotangent[0].astype(jnp.float32) * kept * slope).astype(jnp.bfloat16)
    local_weight = lax.dot_general(
        summed, grad_pre, (((0,), (0,)), ((), ())), preferred_element_type=jnp.float32
    )
    local_bias = jnp.sum(grad_pre.astype(jnp.float32), axis=0)
    grad_weight, grad_bias = lax.psum((local_weight, local_bias), ("row", "col"))
    scale = 1.0 / math.sqrt(n_row * n_col * rows_dev)
    grad_agg = times_weight_t(grad_pre, weight)
    grad_rows = lax.all_gather(grad_agg[None], "col", axis=1, tiled=True)[0]
    back_source = grad_rows.reshape(n_col * rows_dev // tile_size, tile_size, width)
    back = tile_products(
        own_tiles,
        rows_index,
        cols_index,
        live_count,
        back_source,
        n_row * rows_dev // tile_size,
        True,
    )
    back = back.reshape(n_row * rows_dev, width)
    back = lax.optimization_barrier(back.astype(jnp.bfloat16)).astype(jnp.float32)
    grad_sum = lax.psum_scatter(back.astype(jnp.bfloat16), "row", scatter_dimension=0, tiled=True)
    return (hidden[None], grad_weight * scale, grad_bias * scale, grad_sum[None])


def solution(mesh):
    return jax.shard_map(
        on_device,
        mesh=mesh,
        in_specs=(
            P("col", "row", None),
            P("row", "col", None, None, None),
            P("row", "col", None),
            P("row", "col", None),
            P("row", "col"),
            P(),
            P(),
            P("row", "col", None),
            P("row", "col"),
        ),
        out_specs=(P("row", "col", None), P(), P(), P("col", "row", None)),
        check_vma=False,
    )
```

profile of v0, /device:TPU:16, one launch (start us, length us, event | category | flops | bytes accessed | tf_op | source)
XLA Modules:
  0.0 869.9 jit_solution(1376284081427758743)
XLA Ops:
  7.2 0.0 copy-start
  7.2 0.0 copy-start.4
  7.2 0.0 copy-start.5
  7.2 0.0 copy-start.2
  7.2 0.0 all-gather.4.cloned.1.call-start
  7.3 0.7 all-gather.4.cloned.1.call-update
  7.9 0.0 reduce-scatter.3.cloned.1.call-start
  8.7 77.2 %all-gather.4.cloned.1.call-done = bf16[1,4096,256]{2,1,0:T(8,128)(2,1)} async-done(((bf16[1,128,256]{2,1,0:T(8,128)(2,1)}), bf16[1,4096,256]{2,1,0:T(8,128)(2,1)}) %all-gather.4.cloned.1.call-update) | async-done | bytes 2097168 | tf_op jit(solution)/shard_map/all_gather | solution.py:49
  85.9 1.5 broadcast_in_dim.69
  87.4 0.0 copy-done.4
  87.4 0.0 copy-done.5
  87.4 0.0 copy-done.2
  87.4 6.7 while.20
  87.5 0.7 compare_and_fusion.4
  88.2 2.2 gather_fusion
  90.4 0.4 convolution_select_fusion.4
  90.7 0.1 compare_select_fusion.8
  90.8 3.3 scatter_fusion
  94.1 0.0 copy-start.8
  94.1 0.0 copy-start.6
  94.1 0.0 copy-start.7
  94.1 2.7 convert_element_type.42
  96.8 0.0 reduce-scatter.3.cloned.1.call-update
  96.9 0.0 all-gather.6.cloned.1.call-start
  96.9 0.0 copy-done.8
  96.9 122.7 %reduce-scatter.3.cloned.1.call-done = bf16[128,256]{1,0:T(8,128)(2,1)} async-done(((bf16[2048,256]{1,0:T(8,128)(2,1)}), bf16[128,256]{1,0:T(8,128)(2,1)}) %reduce-scatter.3.cloned.1.call-update) | async-done | bytes 65552 | tf_op jit(solution)/shard_map/reduce_scatter | solution.py:55
  219.6 0.0 copy-done
  219.7 0.0 copy-done.6
  219.7 0.0 copy-done.7
  219.7 1.7 convert_reduce_fusion
  221.3 0.0 copy-start.3
  221.3 0.8 convolution_convert_fusion
  222.2 0.0 all-gather.6.cloned.1.call-update
  222.2 0.0 all-reduce.2.cloned.1.call-start
  222.2 2.9 copy.13
  225.2 0.0 copy-done.3
  225.2 0.9 fusion.16
  226.1 0.0 all-reduce.2.cloned.1.call-update
  226.1 0.0 reduce-scatter.5.cloned.1.call-start
  226.2 54.1 %all-gather.6.cloned.1.call-done = bf16[2048,256]{1,0:T(8,128)(2,1)} async-done(((bf16[128,256]{1,0:T(8,128)(2,1)}), bf16[2048,256]{1,0:T(8,128)(2,1)}) %all-gather.6.cloned.1.call-update) | async-done | bytes 1048592 | tf_op jit(solution)/shard_map/all_gather | solution.py:71
  280.3 0.0 copy-start.1
  280.3 2.4 broadcast_in_dim.71
  282.7 0.0 copy-done.1
  282.7 6.0 while.21
  282.7 0.7 compare_and_fusion.5
  283.4 0.6 gather_fusion.1
  284.0 1.3 convolution_select_fusion.5
  285.3 0.1 compare_select_fusion.9
  285.4 3.3 scatter_fusion.1
  288.7 3.8 convert_element_type.52
  292.5 0.0 reduce-scatter.5.cloned.1.call-update
  292.5 136.9 %psum.15 = f32[256]{0:T(256)S(1)} all-reduce(f32[256]{0:T(256)S(1)} %get-tuple-element.136), channel_id=1, replica_groups=mesh['row'=32,'col'=16] {'row','col'}, use_global_device_ids=true, to_apply=%region_6.7 | all-reduce | flops 256 | bytes 2048 | tf_op jit(solution)/shard_map/psum | solution.py:68
  429.4 0.6 broadcast_multiply_fusion.1
  430.0 322.5 %all-reduce.2.cloned.1.call-done = f32[256,256]{1,0:T(8,128)} async-done(((f32[256,256]{1,0:T(8,128)}), f32[256,256]{1,0:T(8,128)}) %all-reduce.2.cloned.1.call-update) | async-done | bytes 262160 | tf_op jit(solution)/shard_map/psum | solution.py:68
  752.5 1.7 broadcast_multiply_fusion
  754.2 109.2 %reduce-scatter.5.cloned.1.call-done = bf16[128,256]{1,0:T(8,128)(2,1)} async-done(((bf16[4096,256]{1,0:T(8,128)(2,1)}), bf16[128,256]{1,0:T(8,128)(2,1)}) %reduce-scatter.5.cloned.1.call-update) | async-done | bytes 65552 | tf_op jit(solution)/shard_map/reduce_scatter | solution.py:84
  (3 shorter events, 0.0 us)
Async XLA Ops:
  7.2 212.5 %copy-start = (bf16[256,256]{1,0:T(8,128)(2,1)S(1)}, bf16[256,256]{1,0:T(8,128)(2,1)}, u32[]{:S(2)}) copy-start(bf16[256,256]{1,0:T(8,128)(2,1)} %param.18) | copy-start | bytes 393220
  7.2 80.3 %copy-start.4 = (s32[1,1,56]{2,1,0:T(1,128)S(1)}, s32[1,1,56]{2,1,0:T(1,128)}, u32[]{:S(2)}) copy-start(s32[1,1,56]{2,1,0:T(1,128)} %param.15) | copy-start | bytes 676
  7.2 80.2 %copy-start.5 = (s32[1,1,56]{2,1,0:T(1,128)S(1)}, s32[1,1,56]{2,1,0:T(1,128)}, u32[]{:S(2)}) copy-start(s32[1,1,56]{2,1,0:T(1,128)} %param.16) | copy-start | bytes 676
  7.2 80.2 %copy-start.2 = (bf16[1,1,56,128,128]{4,3,2,1,0:T(8,128)(2,1)S(1)}, bf16[1,1,56,128,128]{4,3,2,1,0:T(8,128)(2,1)}, u32[]{:S(2)}) copy-start(bf16[1,1,56,128,128]{4,3,2,1,0:T(8,128)(2,1)} %param.14) | copy-start | bytes 5505028
  7.2 78.7 %all-gather.4.cloned.1.call-start = ((), (), s32[]{:S(2)}) async-start(), calls=%async_computation.2 | async-start | bytes 2162688 | tf_op jit(solution)/shard_map/all_gather | solution.py:49
  7.9 211.7 %reduce-scatter.3.cloned.1.call-start = ((), (), s32[]{:S(2)}) async-start(), calls=%async_computation.3 | async-start | bytes 1114112 | tf_op jit(solution)/shard_map/reduce_scatter | solution.py:55
  94.1 2.8 copy-start.8
  94.1 125.5 %copy-start.6 = (bf16[1,128,256]{2,1,0:T(8,128)(2,1)S(1)}, bf16[1,128,256]{2,1,0:T(8,128)(2,1)}, u32[]{:S(2)}) copy-start(bf16[1,128,256]{2,1,0:T(8,128)(2,1)} %param.20) | copy-start | bytes 196612
  94.1 125.5 %copy-start.7 = (f32[256]{0:T(256)S(1)}, f32[256]{0:T(256)}, u32[]{:S(2)}) copy-start(f32[256]{0:T(256)} %param.19) | copy-start | bytes 3076
  96.9 183.4 %all-gather.6.cloned.1.call-start = ((), (), s32[]{:S(2)}) async-start(), calls=%async_computation.6 | async-start | bytes 1114112 | tf_op jit(solution)/shard_map/all_gather | solution.py:71
  221.3 3.8 copy-start.3
  222.2 530.3 %all-reduce.2.cloned.1.call-start = ((), (), s32[]{:S(2)}) async-start(), calls=%async_computation.4 | async-start | bytes 524288 | tf_op jit(solution)/shard_map/psum | solution.py:68
  226.1 637.3 %reduce-scatter.5.cloned.1.call-start = ((), (), s32[]{:S(2)}) async-start(), calls=%async_computation.5 | async-start | bytes 2162688 | tf_op jit(solution)/shard_map/reduce_scatter | solution.py:84
  280.3 2.4 copy-start.1
Sparse Core Ops, SparseCore 0:
  10.1 75.7 all-gather.3
  97.0 122.6 reduce-scatter.2
  223.2 56.9 all-gather.5
  286.1 466.3 all-reduce.1
  755.7 107.6 reduce-scatter.4
where the time goes:
time: 871 us; the launch traced here: 870 us
  waiting for transfers between devices  687 us (79%)
  blocking collectives  137 us (16%)
  other arithmetic  16.9 us (2%)
  between operations  14.5 us (2%)
  local copies, waits for them, and re-layouts  9.66 us (1%)
    psum x1, waiting for transfers between devices, on_device(): lax.psum((local_weight, local_bias), ('row', 'col'))  323 us
    psum x1, blocking collectives, on_device(): lax.psum((local_weight, local_bias), ('row', 'col'))  137 us
    reduce_scatter x1, waiting for transfers between devices, on_device(): lax.psum_scatter(partial_value.astype(jnp.bfloat16), 'col', scatter_dimen...  123 us
    reduce_scatter x1, waiting for transfers between devices, on_device(): lax.psum_scatter(back.astype(jnp.bfloat16), 'row', scatter_dimension=0, t...  109 us
    all_gather x1, waiting for transfers between devices, on_device(): gathered = lax.all_gather(features, 'row', axis=1, tiled=True)  77.2 us
    all_gather x1, waiting for transfers between devices, on_device(): grad_rows = lax.all_gather(grad_agg[None], 'col', axis=1, tiled=True)[0]  54.1 us
  transfers between devices with their start and end apart: 5, of which 5 were waited for; matrix products, arithmetic and copies ran while one was open for 2% of the time, Pallas kernels for 0%

commit v1 on v0

--- a/solution.py
+++ b/solution.py
@@ -65,7 +65,7 @@
         summed, grad_pre, (((0,), (0,)), ((), ())), preferred_element_type=jnp.float32
     )
     local_bias = jnp.sum(grad_pre.astype(jnp.float32), axis=0)
-    grad_weight, grad_bias = lax.psum((local_weight, local_bias), ("row", "col"))
+    grad_weight, grad_bias = lax.psum(lax.psum((local_weight, local_bias), "row"), "col")
     scale = 1.0 / math.sqrt(n_row * n_col * rows_dev)
     grad_agg = times_weight_t(grad_pre, weight)
     grad_rows = lax.all_gather(grad_agg[None], "col", axis=1, tiled=True)[0]

time: 871 us -> 736 us (0.85)
  the two profiles are of different devices: /device:TPU:16 before, /device:TPU:4 now
where the time goes in v1:
time: 736 us; the launch traced here: 734 us
  waiting for transfers between devices  555 us (75%)
  blocking collectives  93.6 us (13%)
  other arithmetic  41.7 us (6%)
  local copies, waits for them, and re-layouts  17.9 us (2%)
  between operations  14.8 us (2%)
  matrix products  11 us (1%)
    psum x1, waiting for transfers between devices, on_device(): lax.psum((local_weight, local_bias), 'row')  206 us
    reduce_scatter x1, waiting for transfers between devices, on_device(): lax.psum_scatter(back.astype(jnp.bfloat16), 'row', scatter_dimension=0, t...  107 us
    reduce_scatter x1, waiting for transfers between devices, on_device(): lax.psum_scatter(partial_value.astype(jnp.bfloat16), 'col', scatter_dimen...  103 us
    all_gather x1, waiting for transfers between devices, on_device(): gathered = lax.all_gather(features, 'row', axis=1, tiled=True)  77.4 us
    all_gather x1, waiting for transfers between devices, on_device(): grad_rows = lax.all_gather(grad_agg[None], 'col', axis=1, tiled=True)[0]  60.7 us
    psum x1, blocking collectives, on_device(): lax.psum((local_weight, local_bias), 'row')  50.7 us
    psum x1, blocking collectives, on_device(): lax.psum(lax.psum((local_weight, local_bias), 'row'), 'col')  42.9 us
    scatter-add x8, other arithmetic, step(): return accum.at[put].add(product)  26.4 us
  transfers between devices with their start and end apart: 6, of which 5 were waited for; matrix products, arithmetic and copies ran while one was open for 5% of the time, Pallas kernels for 0%

profile of v1, /device:TPU:4, one launch (start us, length us, event | category | flops | bytes accessed | tf_op | source)
XLA Modules:
  0.0 734.5 jit_solution(2885548586579943033)
XLA Ops:
  7.3 0.7 all-gather.4.cloned.1.call-update
  7.9 0.0 reduce-scatter.3.cloned.1.call-start
  8.7 77.4 %all-gather.4.cloned.1.call-done = bf16[1,4096,256]{2,1,0:T(8,128)(2,1)} async-done(((bf16[1,128,256]{2,1,0:T(8,128)(2,1)}), bf16[1,4096,256]{2,1,0:T(8,128)(2,1)}) %all-gather.4.cloned.1.call-update) | async-done | bytes 2097168 | tf_op jit(solution)/shard_map/all_gather | solution.py:49
  86.0 1.5 broadcast_in_dim.69
  87.6 26.7 %while.20 = (s32[]{:T(128)}, f32[16,128,256]{2,1,0:T(8,128)}, s32[]{:T(128)}, s32[56]{0:T(128)S(1)}, s32[]{:T(128)}, /*index=5*/bf16[56,128,128]{2,1,0:T(8,128)(...) while((s32[]{:T(128)}, f32[16,128,256]{2,1,0:T(8,128)}, ...), condition=%wide.region_2.3_spmd, body=%wide.region_0.2_spmd.sunk | while | flops 67896416 | bytes 6034855 | solution.py:28
  87.6 0.7 compare_and_fusion.4
  88.3 2.2 gather_fusion
  90.5 0.4 convolution_select_fusion.4
  90.9 0.1 compare_select_fusion.8
  91.0 3.2 scatter_fusion
  94.2 0.7 compare_and_fusion.4
  94.9 2.2 gather_fusion
  97.1 0.4 convolution_select_fusion.4
  97.5 0.1 compare_select_fusion.8
  97.5 3.3 scatter_fusion
  100.8 0.7 compare_and_fusion.4
  101.6 2.2 gather_fusion
  103.7 0.4 convolution_select_fusion.4
  104.1 0.1 compare_select_fusion.8
  104.2 3.3 scatter_fusion
  107.5 0.7 compare_and_fusion.4
  108.3 2.2 gather_fusion
  110.5 0.4 convolution_select_fusion.4
  110.8 0.1 compare_select_fusion.8
  110.9 3.3 scatter_fusion
  114.2 2.7 convert_element_type.42
  117.0 0.0 all-reduce.3.cloned.1.call-start
  117.1 102.7 %reduce-scatter.3.cloned.1.call-done = bf16[128,256]{1,0:T(8,128)(2,1)} async-done(((bf16[2048,256]{1,0:T(8,128)(2,1)}), bf16[128,256]{1,0:T(8,128)(2,1)}) %reduce-scatter.3.cloned.1.call-update) | async-done | bytes 65552 | tf_op jit(solution)/shard_map/reduce_scatter | solution.py:55
  219.8 1.7 convert_reduce_fusion
  221.5 1.8 fusion.16
  223.3 0.0 all-gather.6.cloned.1.call-start
  223.3 0.8 convolution_convert_fusion
  224.2 0.0 all-reduce.5.cloned.1.call-start
  224.2 2.9 copy.13
  227.2 206.4 %all-reduce.3.cloned.1.call-done = f32[256,256]{1,0:T(8,128)} async-done(((f32[256,256]{1,0:T(8,128)}), f32[256,256]{1,0:T(8,128)}) %all-reduce.3.cloned.1.call-update) | async-done | bytes 262160 | tf_op jit(solution)/shard_map/psum | solution.py:68
  433.6 60.7 %all-gather.6.cloned.1.call-done = bf16[2048,256]{1,0:T(8,128)(2,1)} async-done(((bf16[128,256]{1,0:T(8,128)(2,1)}), bf16[2048,256]{1,0:T(8,128)(2,1)}) %all-gather.6.cloned.1.call-update) | async-done | bytes 1048592 | tf_op jit(solution)/shard_map/all_gather | solution.py:71
  494.4 2.4 broadcast_in_dim.71
  496.8 24.2 %while.21 = (s32[]{:T(128)}, f32[32,128,256]{2,1,0:T(8,128)}, s32[]{:T(128)}, s32[56]{0:T(128)S(1)}, s32[]{:T(128)}, /*index=5*/bf16[56,128,128]{1,2,0:T(8,128)(...) while((s32[]{:T(128)}, f32[32,128,256]{2,1,0:T(8,128)}, ...), condition=%wide.region_11.12_spmd, body=%wide.region_9.11_spmd.sunk | while | flops 67896416 | bytes 6033847 | solution.py:28
  496.8 0.7 compare_and_fusion.5
  497.5 0.6 gather_fusion.1
  498.1 1.3 convolution_select_fusion.5
  499.4 0.1 compare_select_fusion.9
  499.5 3.3 scatter_fusion.1
  502.9 0.7 compare_and_fusion.5
  503.6 0.6 gather_fusion.1
  504.2 1.3 convolution_select_fusion.5
  505.5 0.1 compare_select_fusion.9
  505.6 3.3 scatter_fusion.1
  508.9 0.7 compare_and_fusion.5
  509.6 0.6 gather_fusion.1
  510.2 1.3 convolution_select_fusion.5
  511.5 0.1 compare_select_fusion.9
  511.6 3.4 scatter_fusion.1
  515.0 0.7 compare_and_fusion.5
  515.7 0.6 gather_fusion.1
  516.3 1.3 convolution_select_fusion.5
  517.6 0.1 compare_select_fusion.9
  517.7 3.3 scatter_fusion.1
  521.0 3.8 convert_element_type.52
  524.8 50.7 %psum.30 = f32[256]{0:T(256)S(1)} all-reduce(f32[256]{0:T(256)S(1)} %get-tuple-element.136), channel_id=1, replica_groups=mesh['row'=32,'col'=16] {'row'}, use_global_device_ids=true, to_apply=%region_7.8 | all-reduce | flops 256 | bytes 2048 | tf_op jit(solution)/shard_map/psum | solution.py:68
  575.5 42.9 %psum.31 = f32[256]{0:T(256)S(1)} all-reduce(f32[256]{0:T(256)S(1)} %psum.30), channel_id=1, replica_groups=mesh['row'=32,'col'=16] {'col'}, use_global_device_ids=true, to_apply=%region_8.9 | all-reduce | flops 256 | bytes 2048 | tf_op jit(solution)/shard_map/psum | solution.py:68
  618.4 0.6 broadcast_multiply_fusion.1
  619.0 1.7 broadcast_multiply_fusion
  620.7 106.9 %reduce-scatter.5.cloned.1.call-done = bf16[128,256]{1,0:T(8,128)(2,1)} async-done(((bf16[4096,256]{1,0:T(8,128)(2,1)}), bf16[128,256]{1,0:T(8,128)(2,1)}) %reduce-scatter.5.cloned.1.call-update) | async-done | bytes 65552 | tf_op jit(solution)/shard_map/reduce_scatter | solution.py:84
  (33 shorter events, 0.2 us)
Async XLA Ops:
  7.2 212.6 %copy-start = (bf16[256,256]{1,0:T(8,128)(2,1)S(1)}, bf16[256,256]{1,0:T(8,128)(2,1)}, u32[]{:S(2)}) copy-start(bf16[256,256]{1,0:T(8,128)(2,1)} %param.18) | copy-start | bytes 393220
  7.2 80.4 %copy-start.3 = (s32[1,1,56]{2,1,0:T(1,128)S(1)}, s32[1,1,56]{2,1,0:T(1,128)}, u32[]{:S(2)}) copy-start(s32[1,1,56]{2,1,0:T(1,128)} %param.15) | copy-start | bytes 676
  7.2 80.4 %copy-start.4 = (s32[1,1,56]{2,1,0:T(1,128)S(1)}, s32[1,1,56]{2,1,0:T(1,128)}, u32[]{:S(2)}) copy-start(s32[1,1,56]{2,1,0:T(1,128)} %param.16) | copy-start | bytes 676
  7.2 80.4 %copy-start.2 = (bf16[1,1,56,128,128]{4,3,2,1,0:T(8,128)(2,1)S(1)}, bf16[1,1,56,128,128]{4,3,2,1,0:T(8,128)(2,1)}, u32[]{:S(2)}) copy-start(bf16[1,1,56,128,128]{4,3,2,1,0:T(8,128)(2,1)} %param.14) | copy-start | bytes 5505028
  7.2 78.8 %all-gather.4.cloned.1.call-start = ((), (), s32[]{:S(2)}) async-start(), calls=%async_computation.2 | async-start | bytes 2162688 | tf_op jit(solution)/shard_map/all_gather | solution.py:49
  7.9 211.9 %reduce-scatter.3.cloned.1.call-start = ((), (), s32[]{:S(2)}) async-start(), calls=%async_computation.3 | async-start | bytes 1114112 | tf_op jit(solution)/shard_map/reduce_scatter | solution.py:55
  114.2 2.8 copy-start.7
  114.2 105.6 %copy-start.5 = (bf16[1,128,256]{2,1,0:T(8,128)(2,1)S(1)}, bf16[1,128,256]{2,1,0:T(8,128)(2,1)}, u32[]{:S(2)}) copy-start(bf16[1,128,256]{2,1,0:T(8,128)(2,1)} %param.20) | copy-start | bytes 196612
  114.2 105.6 %copy-start.6 = (f32[256]{0:T(256)S(1)}, f32[256]{0:T(256)}, u32[]{:S(2)}) copy-start(f32[256]{0:T(256)} %param.19) | copy-start | bytes 3076
  117.0 316.6 %all-reduce.3.cloned.1.call-start = ((), (), s32[]{:S(2)}) async-start(), calls=%async_computation.4 | async-start | bytes 524288 | tf_op jit(solution)/shard_map/psum | solution.py:68
  223.3 271.1 %all-gather.6.cloned.1.call-start = ((), (), s32[]{:S(2)}) async-start(), calls=%async_computation.7 | async-start | bytes 1114112 | tf_op jit(solution)/shard_map/all_gather | solution.py:71
  224.2 394.8 %all-reduce.5.cloned.1.call-start = ((), (), s32[]{:S(2)}) async-start(), calls=%async_computation.5 | async-start | bytes 524288 | tf_op jit(solution)/shard_map/psum | solution.py:68
  433.6 294.0 %reduce-scatter.5.cloned.1.call-start = ((), (), s32[]{:S(2)}) async-start(), calls=%async_computation.6 | async-start | bytes 2162688 | tf_op jit(solution)/shard_map/reduce_scatter | solution.py:84
  494.4 2.4 copy-start.1
Sparse Core Ops, SparseCore 0:
  10.1 75.8 all-gather.3
  117.1 102.6 reduce-scatter.2
  223.4 210.0 all-reduce.2
  437.0 57.3 all-gather.5
  497.4 114.6 all-reduce.4
  615.3 112.2 reduce-scatter.4
